TPU v7x, 32 devices: a whole 2x2x4 slice. The times are simulated.
32 devices in a mesh: rows: 4 (over y, x), seq: 8 (over z, core).
Axes of the slice: x: 2, y: 2, z: 4, core: 2. Of those that a mesh axis runs over, the one named last changes fastest.
Arguments:
- residual_in: float32 [32, 1024, 512], P('rows', 'seq'), may hold values from -6 to 6
- cotangent: float32 [32, 1024, 512], P('rows', 'seq'), may hold values from -6 to 6
- segments: int32 [32, 1024], P('rows'), may hold values from 0 to 7, never falling along the last dimension, each value on 1 to 512 neighbouring positions
- owners: int32 [96], replicated, may hold values from 0 to 7, as said below
- master_tiles: float32 [128, 512, 128], P('seq'), may hold values from -0.53033009 to 0.53033009, as said below
- first_tiles: float32 [128, 512, 128], P('seq'), may hold values from -0.0024414062 to 0.0024414062
- second_tiles: float32 [128, 512, 128], P('seq'), may hold values from 1.5873903e-07 to 6.349561e-07
- norm_params: float32 [8, 512], replicated, may hold values from -2 to 2
- norm_first: float32 [8, 512], replicated, may hold values from -0.009765625 to 0.009765625
- norm_second: float32 [8, 512], replicated, may hold values from 2.5398244e-06 to 1.0159298e-05
Outputs:
- residual_out: float32 [32, 1024, 512], P('rows', 'seq')
- input_grad: float32 [32, 1024, 512], P('rows', 'seq')
- tile_grads: float32 [128, 512, 128], P('seq')
- grad_norm: float32 [1], replicated
- new_first: float32 [128, 512, 128], P('seq')
- new_second: float32 [128, 512, 128], P('seq')
- new_master: float32 [128, 512, 128], P('seq')
- new_copies: bfloat16 [128, 512, 128], P('seq')
- norm_grads: float32 [8, 512], replicated
- new_norm_first: float32 [8, 512], replicated
- new_norm_second: float32 [8, 512], replicated
- new_norm_params: float32 [8, 512], replicated
Inputs may be any that keep to these rules, and one draw needn't show every extreme that they name: `owners`: no device owns more than 16 tiles, and one device owns exactly 16. `segments`: along a row the document numbers never fall; a document has 1 to 512 positions and some document exactly 512. `master_tiles`: slot 16 d + n holds the tile with the n-th smallest number among those owned by device d; slots that hold no tile are ignored.
All inputs are finite; a program needn't handle non-finite values.
Results may differ from a plain program's by a relative error of at most 0.013.
Values may be sent and summed in bfloat16 or wider, within the bound.
A program may use at most 256 MiB of HBM per device.

v0:
```python
import jax
import jax.numpy as jnp
from jax import lax
from jax.sharding import PartitionSpec as P

HEADS = 8
LAYERS = 2
STEP = 5


def norm_layer(values, gain, offset):
    center = values - jnp.mean(values, axis=-1, keepdims=True)
    spread = jnp.mean(center * center, axis=-1, keepdims=True)
    return center * lax.rsqrt(spread + 1e-05) * gain + offset


def matmul(left, right):
    return jnp.dot(left, right, preferred_element_type=jnp.float32)


def left_product(left, right):
    return lax.dot_general(
        left, right, (((0,), (0,)), ((), ())), preferred_element_type=jnp.float32
    )


def right_product(left, right):
    return lax.dot_general(
        left, right, (((1,), (1,)), ((), ())), preferred_element_type=jnp.float32
    )


def assemble(weight_tiles, layer_number):
    first_tile = 48 * layer_number
    model_width = weight_tiles.shape[1]
    qkv_weight = (
        weight_tiles[first_tile : first_tile + 12].transpose(1, 0, 2).reshape(model_width, -1)
    )
    out_weight = (
        weight_tiles[first_tile + 12 : first_tile + 16].transpose(1, 0, 2).reshape(model_width, -1)
    )
    up_weight = (
        weight_tiles[first_tile + 16 : first_tile + 32].transpose(1, 0, 2).reshape(model_width, -1)
    )
    down_block = weight_tiles[first_tile + 32 : first_tile + 48].reshape(4, 4, model_width, -1)
    down_weight = down_block.transpose(0, 2, 1, 3).reshape(4 * model_width, model_width)
    return (qkv_weight, out_weight, up_weight, down_weight)


def split_tiles(qkv_grad, out_grad, up_grad, down_grad, tile_width):
    model_width = qkv_grad.shape[0]
    pieces = [
        qkv_grad.reshape(model_width, -1, tile_width).transpose(1, 0, 2),
        out_grad.reshape(model_width, -1, tile_width).transpose(1, 0, 2),
        up_grad.reshape(model_width, -1, tile_width).transpose(1, 0, 2),
        down_grad.reshape(4, model_width, 4, tile_width)
        .transpose(0, 2, 1, 3)
        .reshape(16, model_width, tile_width),
    ]
    return jnp.concatenate(pieces, axis=0)


def attend_forward(queries, key_rows, value_rows, doc_ids, block_rows, scale):
    length = queries.shape[0]

    def one_block(number):
        first_row = number * block_rows
        query_block = lax.dynamic_slice_in_dim(queries, first_row, block_rows, 0)
        doc_block = lax.dynamic_slice_in_dim(doc_ids, first_row, block_rows, 0)
        same_doc = doc_block[:, None] == doc_ids[None, :]
        scores = jnp.where(same_doc, right_product(query_block, key_rows) * scale, -1e30)
        largest = jnp.max(scores, axis=-1, keepdims=True)
        row_total = jnp.sum(jnp.exp(scores - largest), axis=-1, keepdims=True)
        logsum = largest + jnp.log(row_total)
        weights = jnp.where(same_doc, jnp.exp(scores - logsum), 0.0).astype(jnp.bfloat16)
        return (matmul(weights, value_rows).astype(jnp.bfloat16), logsum[:, 0])

    outputs, logsums = lax.map(one_block, jnp.arange(length // block_rows))
    return (outputs.reshape(length, -1), logsums.reshape(length))


def attend_backward(queries, key_rows, value_rows, doc_ids, logsums, out_grads, block_rows, scale):
    length, head_dim = queries.shape

    def one_block(carry, number):
        key_grad, value_grad = carry
        first_row = number * block_rows
        query_block = lax.dynamic_slice_in_dim(queries, first_row, block_rows, 0)
        doc_block = lax.dynamic_slice_in_dim(doc_ids, first_row, block_rows, 0)
        logsum_block = lax.dynamic_slice_in_dim(logsums, first_row, block_rows, 0)
        grad_block = lax.dynamic_slice_in_dim(out_grads, first_row, block_rows, 0)
        same_doc = doc_block[:, None] == doc_ids[None, :]
        scores = jnp.where(same_doc, right_product(query_block, key_rows) * scale, -1e30)
        probs = jnp.where(same_doc, jnp.exp(scores - logsum_block[:, None]), 0.0)
        prob_grad = right_product(grad_block, value_rows)
        inner_sum = jnp.sum(probs * prob_grad, axis=-1, keepdims=True)
        score_grad = (probs * (prob_grad - inner_sum)).astype(jnp.bfloat16)
        query_grad = matmul(score_grad, key_rows) * scale
        key_grad = key_grad + left_product(score_grad, query_block) * scale
        value_grad = value_grad + left_product(probs.astype(jnp.bfloat16), grad_block)
        return ((key_grad, value_grad), query_grad)

    zeros_block = jnp.zeros((length, head_dim), jnp.float32)
    (key_grad, value_grad), query_grads = lax.scan(
        one_block, (zeros_block, zeros_block), jnp.arange(length // block_rows)
    )
    stacked = jnp.stack([query_grads.reshape(length, head_dim), key_grad, value_grad], axis=1)
    return stacked.astype(jnp.bfloat16)


def adamw(weight, grad, first, second, learn_rate, correction):
    first = 0.5 * first + 0.5 * grad
    second = 0.5 * second + 0.5 * grad * grad
    update = first / correction / (jnp.sqrt(second / correction) + 1e-08)
    return (weight - learn_rate * (update + 0.01 * weight), first, second)


def local(
    residual_in,
    cotangent,
    segments,
    owners,
    master_tiles,
    first_tiles,
    second_tiles,
    norm_params,
    norm_first,
    norm_second,
):
    local_rows, positions, model_width = residual_in.shape
    seq_devices = lax.axis_size("seq")
    seq_index = lax.axis_index("seq")
    head_dim = model_width // HEADS
    group_count = seq_devices // HEADS
    group_rows = local_rows // group_count
    length = positions * seq_devices
    block_rows = min(512, length)
    scale = head_dim ** (-0.5)
    tile_total = owners.shape[0]
    capacity = master_tiles.shape[0]
    tile_width = master_tiles.shape[2]
    places = jnp.arange(tile_total, dtype=jnp.int32)
    before = (owners[None, :] == owners[:, None]) & (places[None, :] < places[:, None])
    ranks = jnp.sum(before.astype(jnp.int32), axis=1)
    slot_ids = owners * capacity + ranks
    local_slots = jnp.arange(capacity, dtype=jnp.int32)
    matches = (owners[:, None] == seq_index) & (ranks[:, None] == local_slots[None, :])
    chosen = jnp.sum(jnp.where(matches, places[:, None], 0), axis=0)
    present = jnp.any(matches, axis=0)
    copies = lax.all_gather(master_tiles.astype(jnp.bfloat16), "seq", axis=0, tiled=True)
    weight_tiles = jnp.take(copies, slot_ids, axis=0)
    my_group = seq_index // HEADS
    doc_rows = lax.dynamic_slice_in_dim(segments, my_group * group_rows, group_rows, 0)
    hidden = residual_in.reshape(-1, model_width)
    saved = []
    for layer_number in range(LAYERS):
        qkv_weight, out_weight, up_weight, down_weight = assemble(weight_tiles, layer_number)
        params = norm_params[4 * layer_number : 4 * layer_number + 4]
        normed, first_pull = jax.vjp(norm_layer, hidden, params[0], params[1])
        normed_low = normed.astype(jnp.bfloat16)
        packed = matmul(normed_low, qkv_weight).astype(jnp.bfloat16)
        outgoing = packed.reshape(group_count, group_rows, positions, 3, HEADS, head_dim)
        outgoing = outgoing.transpose(0, 4, 1, 2, 3, 5).reshape(
            seq_devices, group_rows, positions * 3 * head_dim
        )
        arrived = lax.all_to_all(outgoing, "seq", split_axis=0, concat_axis=2, tiled=True).reshape(
            group_rows, length, 3, head_dim
        )

        def forward_item(items):
            return attend_forward(
                items[0][:, 0], items[0][:, 1], items[0][:, 2], items[1], block_rows, scale
            )

        attended, logsums = lax.map(forward_item, (arrived, doc_rows))
        returning = attended.reshape(1, group_rows, seq_devices, positions * head_dim)
        mixed = lax.all_to_all(returning, "seq", split_axis=2, concat_axis=0, tiled=True)
        mixed = (
            mixed.reshape(group_count, HEADS, group_rows, positions, head_dim)
            .transpose(0, 2, 3, 1, 4)
            .reshape(-1, model_width)
        )
        middle = hidden + matmul(mixed, out_weight)
        normed_two, second_pull = jax.vjp(norm_layer, middle, params[2], params[3])
        normed_two_low = normed_two.astype(jnp.bfloat16)
        inner = matmul(normed_two_low, up_weight)
        active = jax.nn.gelu(inner).astype(jnp.bfloat16)
        hidden = middle + matmul(active, down_weight)
        saved.append(
            (
                first_pull,
                normed_low,
                arrived,
                logsums,
                mixed,
                second_pull,
                normed_two_low,
                inner,
                active,
            )
        )
    grad = cotangent.reshape(-1, model_width)
    tile_parts = [None] * LAYERS
    norm_parts = [None] * LAYERS
    for layer_number in reversed(range(LAYERS)):
        (
            first_pull,
            normed_low,
            arrived,
            logsums,
            mixed,
            second_pull,
            normed_two_low,
            inner,
            active,
        ) = saved[layer_number]
        qkv_weight, out_weight, up_weight, down_weight = assemble(weight_tiles, layer_number)
        grad_low = grad.astype(jnp.bfloat16)
        down_grad = left_product(active, grad_low)
        active_grad = right_product(grad_low, down_weight)
        inner_grad = jax.vjp(jax.nn.gelu, inner)[1](active_grad)[0].astype(jnp.bfloat16)
        up_grad = left_product(normed_two_low, inner_grad)
        middle_part, gain_two, offset_two = second_pull(right_product(inner_grad, up_weight))
        middle_grad = grad + middle_part
        middle_low = middle_grad.astype(jnp.bfloat16)
        out_grad = left_product(mixed, middle_low)
        mixed_grad = right_product(middle_low, out_weight).astype(jnp.bfloat16)
        sending = mixed_grad.reshape(group_count, group_rows, positions, HEADS, head_dim)
        sending = sending.transpose(0, 3, 1, 2, 4).reshape(
            seq_devices, group_rows, positions * head_dim
        )
        head_grads = lax.all_to_all(
            sending, "seq", split_axis=0, concat_axis=2, tiled=True
        ).reshape(group_rows, length, head_dim)

        def backward_item(items):
            arrived_row, doc_row, logsum_row, grad_row = items
            return attend_backward(
                arrived_row[:, 0],
                arrived_row[:, 1],
                arrived_row[:, 2],
                doc_row,
                logsum_row,
                grad_row,
                block_rows,
                scale,
            )

        packed_grads = lax.map(backward_item, (arrived, doc_rows, logsums, head_grads))
        coming = lax.all_to_all(
            packed_grads.reshape(1, group_rows, seq_devices, positions * 3 * head_dim),
            "seq",
            split_axis=2,
            concat_axis=0,
            tiled=True,
        )
        qkv_grad = coming.reshape(group_count, HEADS, group_rows, positions, 3, head_dim)
        qkv_grad = qkv_grad.transpose(0, 2, 3, 4, 1, 5).reshape(-1, 3 * model_width)
        qkv_weight_grad = left_product(normed_low, qkv_grad)
        input_part, gain_one, offset_one = first_pull(right_product(qkv_grad, qkv_weight))
        grad = middle_grad + input_part
        tile_parts[layer_number] = split_tiles(
            qkv_weight_grad, out_grad, up_grad, down_grad, tile_width
        )
        norm_parts[layer_number] = jnp.stack([gain_one, offset_one, gain_two, offset_two])
    dense = jnp.concatenate(tile_parts, axis=0)
    norm_part = jnp.concatenate(norm_parts, axis=0)
    piece = lax.psum_scatter(
        dense.reshape(-1, tile_width), ("rows", "seq"), scatter_dimension=0, tiled=True
    )
    squares, norm_sum = lax.psum((jnp.sum(piece * piece), norm_part), ("rows", "seq"))
    summed = (
        lax.all_gather(piece.astype(jnp.bfloat16), ("rows", "seq"), axis=0, tiled=True)
        .astype(piece.dtype)
        .reshape(dense.shape)
    )
    owned = jnp.take(summed, chosen, axis=0)
    keep = present[:, None, None]
    owned = jnp.where(keep, owned, 0.0)
    total = jnp.sqrt(squares + jnp.sum(norm_sum * norm_sum))
    factor = 1.0 / jnp.maximum(total, 1.0)
    clipped = owned * factor
    norm_clip = norm_sum * factor
    correction = 1.0 - 0.5**STEP
    new_weight, new_first_rows, new_second_rows = adamw(
        master_tiles, clipped, first_tiles, second_tiles, 0.05, correction
    )
    new_weight = jnp.where(keep, new_weight, 0.0)
    new_first_rows = jnp.where(keep, new_first_rows, 0.0)
    new_second_rows = jnp.where(keep, new_second_rows, 0.0)
    new_norm, new_norm_f, new_norm_s = adamw(
        norm_params, norm_clip, norm_first, norm_second, 0.25, correction
    )
    return (
        hidden.reshape(local_rows, positions, model_width),
        grad.reshape(local_rows, positions, model_width),
        clipped,
        total[None],
        new_first_rows,
        new_second_rows,
        new_weight,
        new_weight.astype(jnp.bfloat16),
        norm_clip,
        new_norm_f,
        new_norm_s,
        new_norm,
    )


def solution(mesh):
    placed = (
        P("rows", "seq", None),
        P("rows", "seq", None),
        P("rows", None),
        P(),
        P("seq", None, None),
        P("seq", None, None),
        P("seq", None, None),
        P(),
        P(),
        P(),
    )
    return jax.shard_map(
        local,
        mesh=mesh,
        in_specs=placed,
        out_specs=(
            P("rows", "seq", None),
            P("rows", "seq", None),
            P("seq", None, None),
            P(),
            P("seq", None, None),
            P("seq", None, None),
            P("seq", None, None),
            P("seq", None, None),
            P(),
            P(),
            P(),
            P(),
        ),
        check_vma=False,
    )
```

profile of v0, /device:TPU:0, one launch (start us, length us, event | category | flops | bytes accessed | tf_op | source)
XLA Modules:
  0.0 1696.8 jit_solution(15735014790983426228)
XLA Ops:
  17.2 147.9 %all-gather.3.cloned.1.call-done = bf16[128,512,128]{2,1,0:T(8,128)(2,1)} async-done(((bf16[16,512,128]{2,1,0:T(8,128)(2,1)}), bf16[128,512,128]{2,1,0:T(8,128)(2,1)}) %all-gather.3.cloned.1.call-update) | async-done | bytes 16777232 | tf_op jit(solution)/shard_map/all_gather | solution.py:150
  165.1 12.7 gather_fusion
  202.6 9.9 copy.210
  212.6 10.4 reshape.599
  226.8 71.4 %all-to-all-done = bf16[8,8,24576]{2,1,0:T(8,128)(2,1)S(1)} async-done(((bf16[8,8,24576]{2,1,0:T(8,128)(2,1)}), bf16[8,8,24576]{2,1,0:T(8,128)(2,1)S(1)}, u32[]{:S(2)}, u32[]{:S(2)}) %all-to-all-start) | async-done | bytes 3145760 | tf_op jit(solution)/shard_map/all_to_all | solution.py:166
  301.6 10.4 reshape.600
  320.5 63.0 %while.99 = (s32[]{:T(128)}, bf16[8,1024,64]{2,1,0:T(8,128)(2,1)S(1)}, f32[8,1024]{1,0:T(8,128)S(1)}, bf16[8,1024,3,64]{3,1,2,0:T(8,128)(2,1)}, s32[8,1024]{1,0:...) while((s32[]{:T(128)}, ...), condition=%wide.region_8.9_spmd, body=%wide.region_3.8_spmd.sunk | while | flops 139492864 | bytes 9431484 | solution.py:175
  448.7 10.0 copy.220
  458.7 10.4 reshape.610
  473.9 71.5 %all-to-all-done.2 = bf16[8,8,24576]{2,1,0:T(8,128)(2,1)} async-done(((bf16[8,8,24576]{2,1,0:T(8,128)(2,1)}), bf16[8,8,24576]{2,1,0:T(8,128)(2,1)}, u32[]{:S(2)}, u32[]{:S(2)}) %all-to-all-start.2) | async-done | bytes 3145760 | tf_op jit(solution)/shard_map/all_to_all | solution.py:166
  550.8 10.5 reshape.611
  570.5 69.8 %while.101 = (s32[]{:T(128)}, bf16[8,1024,64]{2,1,0:T(8,128)(2,1)}, f32[8,1024]{1,0:T(8,128)S(1)}, bf16[8,1024,3,64]{3,1,2,0:T(8,128)(2,1)}, s32[8,1024]{1,0:T(8...) while((s32[]{:T(128)}, bf16[8,1024,64]{2,1,0:T(8,128)(2,1)}, ...), condition=%wide.region_18.19_spmd, body=%wide.region_13.18_spmd.sunk | while | flops 139492864 | bytes 9300412 | solution.py:175
  665.0 10.4 all-to-all-done.3
  715.4 26.5 %all-to-all-done.4 = bf16[8,8,8192]{2,1,0:T(8,128)(2,1)S(1)} async-done(((bf16[8,8,8192]{2,1,0:T(8,128)(2,1)}), bf16[8,8,8192]{2,1,0:T(8,128)(2,1)S(1)}, u32[]{:S(2)}, u32[]{:S(2)}) %all-to-all-start.4) | async-done | bytes 1048608 | tf_op jit(solution)/shard_map/all_to_all | solution.py:232
  748.7 104.2 %while.103 = (s32[]{:T(128)}, bf16[8,1024,3,64]{1,3,2,0:T(8,128)(2,1)}, bf16[8,1024,3,64]{3,1,2,0:T(8,128)(2,1)}, s32[8,1024]{1,0:T(8,128)S(1)}, f32[8,1024]{1,0...) while((s32[]{:T(128)}, ...), condition=%wide.region_27.28_spmd, body=%wide.region_23.27_spmd.sunk | while | flops 342982144 | bytes 30577220 | solution.py:249
  751.3 8.7 while.108
  764.3 8.7 while.108
  777.3 8.7 while.108
  790.4 8.7 while.108
  803.4 8.7 while.108
  816.4 8.7 while.108
  829.4 8.7 while.108
  842.4 8.7 while.108
  852.9 12.5 copy.235
  865.4 9.2 reshape.624
  876.4 74.5 %all_to_all.120 = bf16[1,8,8,24576]{3,1,0,2:T(8,128)(2,1)S(1)} all-to-all(bf16[1,8,8,24576]{3,1,0,2:T(8,128)(2,1)S(1)} %copy.236), channel_id=1, replica_groups=mesh['rows'=4,'seq'=8] {'seq'}, dimensions={2} | all-to-all | bytes 6291456 | tf_op jit(solution)/shard_map/all_to_all | solution.py:250
  950.8 8.7 reshape.625
  983.5 10.4 fusion.56
  1016.3 26.5 %all-to-all-done.6 = bf16[8,8,8192]{2,1,0:T(8,128)(2,1)S(1)} async-done(((bf16[8,8,8192]{2,1,0:T(8,128)(2,1)}), bf16[8,8,8192]{2,1,0:T(8,128)(2,1)S(1)}, u32[]{:S(2)}, u32[]{:S(2)}) %all-to-all-start.6) | async-done | bytes 1048608 | tf_op jit(solution)/shard_map/all_to_all | solution.py:232
  1049.6 102.7 %while.105 = (s32[]{:T(128)}, bf16[8,1024,3,64]{1,3,2,0:T(8,128)(2,1)}, bf16[8,1024,3,64]{3,1,2,0:T(8,128)(2,1)}, s32[8,1024]{1,0:T(8,128)S(1)}, f32[8,1024]{1,0...) while((s32[]{:T(128)}, ...), condition=%wide.region_36.37_spmd, body=%wide.region_32.36_spmd.sunk | while | flops 342982144 | bytes 30577220 | solution.py:249
  1077.9 8.5 while.109
  1090.7 8.5 while.109
  1116.4 8.5 while.109
  1129.3 8.5 while.109
  1142.1 8.5 while.109
  1152.4 12.5 copy.244
  1164.9 9.2 reshape.630
  1200.3 9.2 fusion.106
  1228.1 25.8 %all-to-all-done.7 = bf16[1,8,8,24576]{3,1,0,2:T(8,128)(2,1)} async-done(((bf16[1,8,8,24576]{3,1,0,2:T(8,128)(2,1)}), bf16[1,8,8,24576]{3,1,0,2:T(8,128)(2,1)}, u32[]{:S(2)}, u32[]{:S(2)}) %all-to-all-start.7) | async-done | bytes 3145760 | tf_op jit(solution)/shard_map/all_to_all | solution.py:250
  1253.9 10.6 reshape.631
  1264.4 9.5 copy.246
  1302.8 244.3 %reduce-scatter.2.cloned.1.call-done = f32[1536,128]{1,0:T(8,128)} async-done(((f32[49152,128]{1,0:T(8,128)}), f32[1536,128]{1,0:T(8,128)}) %reduce-scatter.2.cloned.1.call-update) | async-done | bytes 786448 | tf_op jit(solution)/shard_map/reduce_scatter | solution.py:268
  1550.3 8.7 fusion.91
  1579.6 42.8 %all-reduce = (f32[]{:T(128)}, f32[8,512]{1,0:T(8,128)S(1)}) all-reduce(f32[]{:T(128)} %get-tuple-element.743, f32[8,512]{1,0:T(8,128)S(1)} %concatenate.23), channel_id=1, replica_groups=mesh['rows'=4,'seq'=8] {'rows','seq'}, use_global_device_ids=true, to_apply=%region_43.44 | all-reduce | flops 4097 | bytes 32776 | tf_op jit(solution)/shard_map/psum | solution.py:271
  1625.1 23.5 %all-gather.5.cloned.1.call-done = bf16[49152,128]{1,0:T(8,128)(2,1)} async-done(((bf16[1536,128]{1,0:T(8,128)(2,1)}), bf16[49152,128]{1,0:T(8,128)(2,1)}) %all-gather.5.cloned.1.call-update) | async-done | bytes 12582928 | tf_op jit(solution)/shard_map/all_gather | solution.py:273
  1648.5 14.2 convert.25
  1662.7 11.0 gather_fusion.1
  1673.7 9.6 fusion.133
  (1360 shorter events, 783.0 us)
Async XLA Ops:
  7.2 157.9 %all-gather.3.cloned.1.call-start = ((), (), s32[]{:S(2)}) async-start(), calls=%async_computation.9 | async-start | bytes 18874368 | tf_op jit(solution)/shard_map/all_gather | solution.py:150
  15.3 410.2 %copy-start.97 = (f32[1,512]{1,0:T(1,128)}, f32[1,512]{1,0:T(1,128)S(1)}, u32[]{:S(2)}) copy-start(f32[1,512]{1,0:T(1,128)S(1)} %get-tuple-element.748) | copy-start | bytes 6148
  15.3 410.2 %copy-start.110 = (f32[1,512]{1,0:T(1,128)}, f32[1,512]{1,0:T(1,128)S(1)}, u32[]{:S(2)}) copy-start(f32[1,512]{1,0:T(1,128)S(1)} %get-tuple-element.747) | copy-start | bytes 6148
  15.3 418.9 %copy-start.94 = (f32[1,512]{1,0:T(1,128)}, f32[1,512]{1,0:T(1,128)S(1)}, u32[]{:S(2)}) copy-start(f32[1,512]{1,0:T(1,128)S(1)} %get-tuple-element.746) | copy-start | bytes 6148
  15.3 418.9 %copy-start.108 = (f32[1,512]{1,0:T(1,128)}, f32[1,512]{1,0:T(1,128)S(1)}, u32[]{:S(2)}) copy-start(f32[1,512]{1,0:T(1,128)S(1)} %get-tuple-element.745) | copy-start | bytes 6148
  222.9 75.3 %all-to-all-start = ((bf16[8,8,24576]{2,1,0:T(8,128)(2,1)}), bf16[8,8,24576]{2,1,0:T(8,128)(2,1)S(1)}, u32[]{:S(2)}, u32[]{:S(2)}) async-start(bf16[8,8,24576]{2,1,0:T(8,128)(2,1)} %reshape.599), calls=%async_computation | async-start | bytes 6291456 | tf_op jit(solution)/shard_map/all_to_all | solution.py:166
  387.4 30.1 %all-to-all-start.1 = ((bf16[1,8,8,8192]{3,1,0,2:T(8,128)(2,1)}), bf16[1,8,8,8192]{3,1,0,2:T(8,128)(2,1)S(1)}, u32[]{:S(2)}, u32[]{:S(2)}) async-start(bf16[1,8,8,8192]{3,1,0,2:T(8,128)(2,1)} %copy.213), calls=%async_computation.1 | async-start | bytes 2097152 | tf_op jit(solution)/shard_map/all_to_all | solution.py:177
  392.9 30.1 %copy-start = (f32[1024,512]{0,1:T(8,128)}, f32[1024,512]{0,1:T(8,128)S(1)}, u32[]{:S(2)}) copy-start(f32[1024,512]{0,1:T(8,128)S(1)} %copy.262) | copy-start | bytes 6291460
  425.1 5.1 copy-start.7
  425.1 5.0 copy-start.71
  425.5 4.7 copy-start.79
  433.8 247.0 %copy-start.2 = (f32[1024,512]{0,1:T(8,128)}, f32[1024,512]{0,1:T(8,128)S(1)}, u32[]{:S(2)}) copy-start(f32[1024,512]{0,1:T(8,128)S(1)} %get-tuple-element.760) | copy-start | bytes 6291460
  433.8 5.9 copy-start.64
  434.1 5.6 copy-start.81
  434.1 5.6 copy-start.76
  469.1 76.4 %all-to-all-start.2 = ((bf16[8,8,24576]{2,1,0:T(8,128)(2,1)}), bf16[8,8,24576]{2,1,0:T(8,128)(2,1)}, u32[]{:S(2)}, u32[]{:S(2)}) async-start(bf16[8,8,24576]{2,1,0:T(8,128)(2,1)} %reshape.610), calls=%async_computation.2 | async-start | bytes 6291456 | tf_op jit(solution)/shard_map/all_to_all | solution.py:166
  645.2 30.2 %all-to-all-start.3 = ((bf16[1,8,8,8192]{3,1,0,2:T(8,128)(2,1)}), bf16[1,8,8,8192]{3,1,0,2:T(8,128)(2,1)S(1)}, u32[]{:S(2)}, u32[]{:S(2)}) async-start(bf16[1,8,8,8192]{3,1,0,2:T(8,128)(2,1)} %copy.223), calls=%async_computation.3 | async-start | bytes 2097152 | tf_op jit(solution)/shard_map/all_to_all | solution.py:177
  682.9 20.3 %copy-start.12 = (f32[1024,512]{0,1:T(8,128)}, f32[1024,512]{0,1:T(8,128)S(1)}, u32[]{:S(2)}) copy-start(f32[1024,512]{0,1:T(8,128)S(1)} %get-tuple-element.762) | copy-start | bytes 6291460
  682.9 20.2 %copy-start.85 = (f32[1024]{0:T(1024)}, f32[1024]{0:T(1024)S(1)}, u32[]{:S(2)}) copy-start(f32[1024]{0:T(1024)S(1)} %broadcast_multiply_fusion.1) | copy-start | bytes 12292
  683.3 19.9 %copy-start.102 = (f32[1024]{0:T(1024)}, f32[1024]{0:T(1024)S(1)}, u32[]{:S(2)}) copy-start(f32[1024]{0:T(1024)S(1)} %fusion.118) | copy-start | bytes 12292
  685.3 6.5 copy-start.47
  685.3 6.5 copy-start.56
  691.8 7.9 copy-start.126
  711.5 30.3 %all-to-all-start.4 = ((bf16[8,8,8192]{2,1,0:T(8,128)(2,1)}), bf16[8,8,8192]{2,1,0:T(8,128)(2,1)S(1)}, u32[]{:S(2)}, u32[]{:S(2)}) async-start(bf16[8,8,8192]{2,1,0:T(8,128)(2,1)} %reshape.622), calls=%async_computation.4 | async-start | bytes 2097152 | tf_op jit(solution)/shard_map/all_to_all | solution.py:232
  967.5 6.3 copy-start.29
  983.5 10.4 copy-start.21
  983.5 10.4 copy-start.49
  1012.7 30.1 %all-to-all-start.6 = ((bf16[8,8,8192]{2,1,0:T(8,128)(2,1)}), bf16[8,8,8192]{2,1,0:T(8,128)(2,1)S(1)}, u32[]{:S(2)}, u32[]{:S(2)}) async-start(bf16[8,8,8192]{2,1,0:T(8,128)(2,1)} %reshape.628), calls=%async_computation.6 | async-start | bytes 2097152 | tf_op jit(solution)/shard_map/all_to_all | solution.py:232
  1177.5 4.9 copy-start.33
  1177.5 76.3 %all-to-all-start.7 = ((bf16[1,8,8,24576]{3,1,0,2:T(8,128)(2,1)}), bf16[1,8,8,24576]{3,1,0,2:T(8,128)(2,1)}, u32[]{:S(2)}, u32[]{:S(2)}) async-start(bf16[1,8,8,24576]{3,1,0,2:T(8,128)(2,1)} %copy.245), calls=%async_computation.7 | async-start | bytes 6291456 | tf_op jit(solution)/shard_map/all_to_all | solution.py:250
  1182.3 364.8 %reduce-scatter.2.cloned.1.call-start = ((), (), s32[]{:S(2)}) async-start(), calls=%async_computation.10 | async-start | bytes 25952256 | tf_op jit(solution)/shard_map/reduce_scatter | solution.py:268
  1184.1 6.6 copy-start.13
  1184.2 6.6 copy-start.86
  1184.2 6.6 copy-start.103
  1184.2 6.6 copy-start.106
  1184.2 6.6 copy-start.113
  1190.8 6.9 copy-start.30
  1214.7 4.8 copy-start.43
  1214.7 4.8 copy-start.55
  1302.7 247.3 %copy-start.120 = (s32[96]{0:T(128)S(1)}, s32[96]{0:T(128)}, u32[]{:S(2)}) copy-start(s32[96]{0:T(128)} %copy-done.119) | copy-start | bytes 1156
  1302.7 247.3 %copy-start.121 = (pred[96]{0:T(512)(128)(4,1)S(1)}, pred[96]{0:T(512)(128)(4,1)}, u32[]{:S(2)}) copy-start(pred[96]{0:T(512)(128)(4,1)} %get-tuple-element.756) | copy-start | bytes 292
  1302.8 345.8 %all-gather.5.cloned.1.call-start = ((), (), s32[]{:S(2)}) async-start(), calls=%async_computation.11 | async-start | bytes 12976128 | tf_op jit(solution)/shard_map/all_gather | solution.py:273
  1576.6 47.8 %copy-start.69 = (f32[8,512]{1,0:T(8,128)S(1)}, f32[8,512]{1,0:T(8,128)}, u32[]{:S(2)}) copy-start(f32[8,512]{1,0:T(8,128)} %param.33) | copy-start | bytes 49156
  1576.6 47.8 %copy-start.100 = (f32[8,512]{1,0:T(8,128)S(1)}, f32[8,512]{1,0:T(8,128)}, u32[]{:S(2)}) copy-start(f32[8,512]{1,0:T(8,128)} %param.35) | copy-start | bytes 49156
  1576.6 47.8 %copy-start.101 = (f32[8,512]{1,0:T(8,128)S(1)}, f32[8,512]{1,0:T(8,128)}, u32[]{:S(2)}) copy-start(f32[8,512]{1,0:T(8,128)} %param.34) | copy-start | bytes 49156
  1673.7 9.6 copy-start.26
  1673.7 10.5 copy-start.27
  1683.4 5.6 copy-start.28
  (117 other events, 273.1 us)
Sparse Core Ops, SparseCore 0:
  11.3 153.7 all-gather.2
  1302.9 244.2 reduce-scatter.1
  1551.2 97.3 all-gather.4
where the time goes:
time: 1710 us; the launch traced here: 1700 us
  waiting for transfers between devices  652 us (38%)
  local copies, waits for them, and re-layouts  502 us (29%)
  matrix products  228 us (13%)
  blocking collectives  117 us (7%)
  other arithmetic  104 us (6%)
  loops' own time  47.6 us (3%)
  starting transfers between devices  28.3 us (2%)
  between operations  18 us (1%)
    reduce_scatter x1, waiting for transfers between devices, local(): lax.psum_scatter(dense.reshape(-1, tile_width), ('rows', 'seq'), scatter_...  244 us
    all_gather x1, waiting for transfers between devices, local(): lax.all_gather(master_tiles.astype(jnp.bfloat16), 'seq', axis=0, tiled=True)  148 us
    all_to_all x2, waiting for transfers between devices, local(): lax.all_to_all(outgoing, 'seq', split_axis=0, concat_axis=2, tiled=True)  143 us
    dot_general x104, matrix products, right_product(): lax.dot_general(left, right, (((1,), (1,)), ((), ())), preferred_element_...  98.8 us
    all_to_all x1, blocking collectives, local(): lax.all_to_all(packed_grads.reshape(1, group_rows, seq_devices, positions...  74.5 us
    dot_general x72, matrix products, matmul(): return jnp.dot(left, right, preferred_element_type=jnp.float32)  69.5 us
    dot_general x72, matrix products, left_product(): lax.dot_general(left, right, (((0,), (0,)), ((), ())), preferred_element_...  59.3 us
    unnamed x257, local copies, waits for them, and re-layouts  54.5 us
  transfers between devices with their start and end apart: 10, of which 10 were waited for; matrix products, arithmetic and copies ran while one was open for 7% of the time, Pallas kernels for 0%

commit v1 on v0

--- a/solution.py
+++ b/solution.py
@@ -147,7 +147,17 @@
     matches = (owners[:, None] == seq_index) & (ranks[:, None] == local_slots[None, :])
     chosen = jnp.sum(jnp.where(matches, places[:, None], 0), axis=0)
     present = jnp.any(matches, axis=0)
-    copies = lax.all_gather(master_tiles.astype(jnp.bfloat16), "seq", axis=0, tiled=True)
+    value = master_tiles.astype(jnp.bfloat16)
+    ways = lax.axis_size("seq")
+    up = [(d, (d + 1) % ways) for d in range(ways)]
+    down = [(d, (d - 1) % ways) for d in range(ways)]
+    earlier, later = ([value], [value])
+    for _ in range(ways // 2):
+        earlier.append(lax.ppermute(earlier[-1], "seq", up))
+    for _ in range((ways - 1) // 2):
+        later.append(lax.ppermute(later[-1], "seq", down))
+    line = jnp.concatenate([*earlier[::-1], *later[1:]], axis=0)
+    copies = jnp.roll(line, (lax.axis_index("seq") - ways // 2) * value.shape[0], axis=0)
     weight_tiles = jnp.take(copies, slot_ids, axis=0)
     my_group = seq_index // HEADS
     doc_rows = lax.dynamic_slice_in_dim(segments, my_group * group_rows, group_rows, 0)

time: 1710 us -> 2010 us (1.18)
  matrix products: 228 us -> 403 us
  local copies, waits for them, and re-layouts: 502 us -> 582 us
    ppermute x0 -> x7, waiting for transfers between devices: none -> 160 us  [the longest x4 160 us: local(): earlier.append(lax.ppermute(earlier[-1], 'seq', up))]
    all_gather x1 -> x0, waiting for transfers between devices: 148 us -> none  [local(): lax.all_gather(master_tiles.astype(jnp.bfloat16), 'seq', axis=0, tiled=True)]
    dot_general x72, matrix products: 59.3 us -> 140 us  [left_product(): lax.dot_general(left, right, (((0,), (0,)), ((), ())), preferred_element_...]
    dot_general x104, matrix products: 98.8 us -> 164 us  [right_product(): lax.dot_general(left, right, (((1,), (1,)), ((), ())), preferred_element_...]
    dot_general x72, matrix products: 69.5 us -> 99.7 us  [matmul(): return jnp.dot(left, right, preferred_element_type=jnp.float32)]
    squeeze x16, local copies, waits for them, and re-layouts: 0.42 us -> 26.8 us  [local(): lax.map(backward_item, (arrived, doc_rows, logsums, head_grads))]
    while x80 -> x48, local copies, waits for them, and re-layouts: 24.7 us -> 0.15 us
    dynamic_slice x32, local copies, waits for them, and re-layouts: 0.3 us -> 24.6 us  [local(): attended, logsums = lax.map(forward_item, (arrived, doc_rows))]
  transfers between devices with their start and end apart: 10 -> 16, of which waited for: 10 -> 13; matrix products, arithmetic and copies ran while one was open for 7% -> 6% of each run, Pallas kernels for 0% -> 0%
where the time goes in v1:
time: 2010 us; the launch traced here: 1990 us
  waiting for transfers between devices  665 us (33%)
  local copies, waits for them, and re-layouts  582 us (29%)
  matrix products  403 us (20%)
  other arithmetic  119 us (6%)
  blocking collectives  117 us (6%)
  loops' own time  46.2 us (2%)
  starting transfers between devices  39.4 us (2%)
    reduce_scatter x1, waiting for transfers between devices, local(): lax.psum_scatter(dense.reshape(-1, tile_width), ('rows', 'seq'), scatter_...  244 us
    dot_general x104, matrix products, right_product(): lax.dot_general(left, right, (((1,), (1,)), ((), ())), preferred_element_...  164 us
    ppermute x4, waiting for transfers between devices, local(): earlier.append(lax.ppermute(earlier[-1], 'seq', up))  160 us
    all_to_all x2, waiting for transfers between devices, local(): lax.all_to_all(outgoing, 'seq', split_axis=0, concat_axis=2, tiled=True)  143 us
    dot_general x72, matrix products, left_product(): lax.dot_general(left, right, (((0,), (0,)), ((), ())), preferred_element_...  140 us
    dot_general x72, matrix products, matmul(): return jnp.dot(left, right, preferred_element_type=jnp.float32)  99.7 us
    unnamed x278, local copies, waits for them, and re-layouts  76 us
    all_to_all x1, blocking collectives, local(): lax.all_to_all(packed_grads.reshape(1, group_rows, seq_devices, positions...  74.2 us
  transfers between devices with their start and end apart: 16, of which 13 were waited for; matrix products, arithmetic and copies ran while one was open for 6% of the time, Pallas kernels for 0%

profile of v1, /device:TPU:0, one launch (start us, length us, event | category | flops | bytes accessed | tf_op | source)
XLA Modules:
  0.0 1990.2 jit_solution(779096706371910155)
XLA Ops:
  10.4 27.8 %collective-permute-done = bf16[16,512,128]{2,1,0:T(8,128)(2,1)S(1)} collective-permute-done((bf16[16,512,128]{2,1,0:T(8,128)(2,1)S(1)}, bf16[16,512,128]{2,1,0:T(8,128)(2,1)S(1)}, u32[]{:S(2)}, u32[]{:S(2)}) %collective-permute-start) | collective-permute-done | bytes 2097184 | tf_op jit(solution)/shard_map/ppermute | solution.py:156
  43.0 45.4 %collective-permute-done.1 = bf16[16,512,128]{2,1,0:T(8,128)(2,1)S(1)} collective-permute-done((bf16[16,512,128]{2,1,0:T(8,128)(2,1)S(1)}, bf16[16,512,128]{2,1,0:T(8,128)(2,1)S(1)}, u32[]{:S(2)}, u32[]{:S(2)}) %collective-permute-start.1) | collective-permute-done | bytes 2097184 | tf_op jit(solution)/shard_map/ppermute | solution.py:156
  93.3 46.4 %collective-permute-done.2 = bf16[16,512,128]{2,1,0:T(8,128)(2,1)} collective-permute-done((bf16[16,512,128]{2,1,0:T(8,128)(2,1)S(1)}, bf16[16,512,128]{2,1,0:T(8,128)(2,1)}, u32[]{:S(2)}, u32[]{:S(2)}) %collective-permute-start.2) | collective-permute-done | bytes 2097184 | tf_op jit(solution)/shard_map/ppermute | solution.py:156
  147.3 40.9 %collective-permute-done.3 = bf16[16,512,128]{2,1,0:T(8,128)(2,1)} collective-permute-done((bf16[16,512,128]{2,1,0:T(8,128)(2,1)}, bf16[16,512,128]{2,1,0:T(8,128)(2,1)}, u32[]{:S(2)}, u32[]{:S(2)}) %collective-permute-start.3) | collective-permute-done | bytes 2097184 | tf_op jit(solution)/shard_map/ppermute | solution.py:156
  220.0 12.7 gather_fusion
  257.6 10.0 copy.210
  267.5 10.4 reshape.599
  281.9 71.4 %all-to-all-done = bf16[8,8,24576]{2,1,0:T(8,128)(2,1)S(1)} async-done(((bf16[8,8,24576]{2,1,0:T(8,128)(2,1)}), bf16[8,8,24576]{2,1,0:T(8,128)(2,1)S(1)}, u32[]{:S(2)}, u32[]{:S(2)}) %all-to-all-start) | async-done | bytes 3145760 | tf_op jit(solution)/shard_map/all_to_all | solution.py:176
  356.8 10.5 reshape.600
  375.8 78.8 %while.99 = (s32[]{:T(128)}, bf16[8,1024,64]{2,1,0:T(8,128)(2,1)S(1)}, f32[8,1024]{1,0:T(8,128)}, bf16[8,1024,3,64]{3,1,2,0:T(8,128)(2,1)}, s32[8,1024]{1,0:T(8,...) while((s32[]{:T(128)}, ...), condition=%wide.region_8.9_spmd, body=%wide.region_3.8_spmd.sunk | while | flops 139492864 | bytes 9431484 | solution.py:185
  519.2 10.0 copy.220
  529.2 10.4 reshape.610
  544.3 71.5 %all-to-all-done.2 = bf16[8,8,24576]{2,1,0:T(8,128)(2,1)} async-done(((bf16[8,8,24576]{2,1,0:T(8,128)(2,1)}), bf16[8,8,24576]{2,1,0:T(8,128)(2,1)}, u32[]{:S(2)}, u32[]{:S(2)}) %all-to-all-start.2) | async-done | bytes 3145760 | tf_op jit(solution)/shard_map/all_to_all | solution.py:176
  621.1 10.5 reshape.611
  640.9 74.6 %while.101 = (s32[]{:T(128)}, bf16[8,1024,64]{2,1,0:T(8,128)(2,1)}, f32[8,1024]{1,0:T(8,128)S(1)}, bf16[8,1024,3,64]{3,1,2,0:T(8,128)(2,1)}, s32[8,1024]{1,0:T(8...) while((s32[]{:T(128)}, bf16[8,1024,64]{2,1,0:T(8,128)(2,1)}, ...), condition=%wide.region_18.19_spmd, body=%wide.region_13.18_spmd.sunk | while | flops 139492864 | bytes 9300412 | solution.py:185
  740.5 10.4 all-to-all-done.3
  790.7 26.5 %all-to-all-done.4 = bf16[8,8,8192]{2,1,0:T(8,128)(2,1)S(1)} async-done(((bf16[8,8,8192]{2,1,0:T(8,128)(2,1)}), bf16[8,8,8192]{2,1,0:T(8,128)(2,1)S(1)}, u32[]{:S(2)}, u32[]{:S(2)}) %all-to-all-start.4) | async-done | bytes 1048608 | tf_op jit(solution)/shard_map/all_to_all | solution.py:242
  823.1 210.7 %while.103 = (s32[]{:T(128)}, bf16[8,1024,3,64]{1,3,2,0:T(8,128)(2,1)}, bf16[8,1024,3,64]{3,1,2,0:T(8,128)(2,1)}, s32[8,1024]{1,0:T(8,128)}, f32[8,1024]{1,0:T(8...) while((s32[]{:T(128)}, ...), condition=%wide.region_27.28_spmd, body=%wide.region_23.27_spmd.sunk | while | flops 342982144 | bytes 22319684 | solution.py:259
  827.7 19.7 while.108
  854.1 19.7 while.108
  880.4 19.7 while.108
  906.7 19.7 while.108
  933.1 19.7 while.108
  959.4 19.7 while.108
  985.7 19.7 while.108
  1012.1 19.7 while.108
  1033.8 12.6 copy.235
  1057.3 74.2 %all_to_all.120 = bf16[1,8,8,24576]{3,1,0,2:T(8,128)(2,1)S(1)} all-to-all(bf16[1,8,8,24576]{3,1,0,2:T(8,128)(2,1)S(1)} %copy.236), channel_id=1, replica_groups=mesh['rows'=4,'seq'=8] {'seq'}, dimensions={2} | all-to-all | bytes 6291456 | tf_op jit(solution)/shard_map/all_to_all | solution.py:260
  1164.3 10.4 fusion.56
  1197.4 26.5 %all-to-all-done.6 = bf16[8,8,8192]{2,1,0:T(8,128)(2,1)S(1)} async-done(((bf16[8,8,8192]{2,1,0:T(8,128)(2,1)}), bf16[8,8,8192]{2,1,0:T(8,128)(2,1)S(1)}, u32[]{:S(2)}, u32[]{:S(2)}) %all-to-all-start.6) | async-done | bytes 1048608 | tf_op jit(solution)/shard_map/all_to_all | solution.py:242
  1229.8 215.8 %while.105 = (s32[]{:T(128)}, bf16[8,1024,3,64]{1,3,2,0:T(8,128)(2,1)}, bf16[8,1024,3,64]{3,1,2,0:T(8,128)(2,1)}, s32[8,1024]{1,0:T(8,128)}, f32[8,1024]{1,0:T(8...) while((s32[]{:T(128)}, ...), condition=%wide.region_36.37_spmd, body=%wide.region_32.36_spmd.sunk | while | flops 342982144 | bytes 22057484 | solution.py:259
  1235.1 19.7 while.109
  1262.1 19.6 while.109
  1289.1 19.7 while.109
  1316.0 19.6 while.109
  1343.0 19.7 while.109
  1370.0 19.6 while.109
  1397.0 19.7 while.109
  1424.0 19.6 while.109
  1445.6 12.6 copy.244
  1521.3 25.6 %all-to-all-done.7 = bf16[1,8,8,24576]{3,1,0,2:T(8,128)(2,1)} async-done(((bf16[1,8,8,24576]{3,1,0,2:T(8,128)(2,1)}), bf16[1,8,8,24576]{3,1,0,2:T(8,128)(2,1)}, u32[]{:S(2)}, u32[]{:S(2)}) %all-to-all-start.7) | async-done | bytes 3145760 | tf_op jit(solution)/shard_map/all_to_all | solution.py:260
  1546.9 10.6 reshape.631
  1595.7 244.2 %reduce-scatter.2.cloned.1.call-done = f32[1536,128]{1,0:T(8,128)} async-done(((f32[49152,128]{1,0:T(8,128)}), f32[1536,128]{1,0:T(8,128)}) %reduce-scatter.2.cloned.1.call-update) | async-done | bytes 786448 | tf_op jit(solution)/shard_map/reduce_scatter | solution.py:278
  1872.6 42.6 %all-reduce = (f32[]{:T(128)}, f32[8,512]{1,0:T(8,128)S(1)}) all-reduce(f32[]{:T(128)} %get-tuple-element.743, f32[8,512]{1,0:T(8,128)S(1)} %concatenate.30), channel_id=1, replica_groups=mesh['rows'=4,'seq'=8] {'rows','seq'}, use_global_device_ids=true, to_apply=%region_43.44 | all-reduce | flops 4097 | bytes 32776 | tf_op jit(solution)/shard_map/psum | solution.py:281
  1917.9 23.5 %all-gather.2.cloned.1.call-done = bf16[49152,128]{1,0:T(8,128)(2,1)} async-done(((bf16[1536,128]{1,0:T(8,128)(2,1)}), bf16[49152,128]{1,0:T(8,128)(2,1)}) %all-gather.2.cloned.1.call-update) | async-done | bytes 12582928 | tf_op jit(solution)/shard_map/all_gather | solution.py:283
  1941.3 14.2 convert.25
  1955.5 11.0 gather_fusion.1
  1966.6 9.6 fusion.133
  (1364 shorter events, 1092.8 us)
Async XLA Ops:
  7.2 132.5 %copy-start.7 = (f32[8,128,512]{2,1,0:T(8,128)S(1)}, f32[8,128,512]{2,1,0:T(8,128)}, u32[]{:S(2)}) copy-start(f32[8,128,512]{2,1,0:T(8,128)} %param.26) | copy-start | bytes 6291460
  9.9 130.0 %copy-start.120 = (s32[96]{0:T(128)S(1)}, s32[96]{0:T(128)}, u32[]{:S(2)}) copy-start(s32[96]{0:T(128)} %param.29) | copy-start | bytes 1156
  9.9 28.3 %collective-permute-start = (bf16[16,512,128]{2,1,0:T(8,128)(2,1)S(1)}, bf16[16,512,128]{2,1,0:T(8,128)(2,1)S(1)}, u32[]{:S(2)}, u32[]{:S(2)}) collective-permute-start(bf16[16,512,128]{2,1,0:T(8,128)(2,1)S(1)} %convert_element_type.116), channel_id=1, source_target_pairs={{0,1},{1,2},{2,3},{3,4},{4,5},{5,6},{6,7},{7,0},{8,9},{9,10},{10,1... | collective-permute-start | bytes 6291464 | tf_op jit(solution)/shard_map/ppermute | solution.py:156
  39.5 49.0 %collective-permute-start.1 = (bf16[16,512,128]{2,1,0:T(8,128)(2,1)S(1)}, bf16[16,512,128]{2,1,0:T(8,128)(2,1)S(1)}, u32[]{:S(2)}, u32[]{:S(2)}) collective-permute-start(bf16[16,512,128]{2,1,0:T(8,128)(2,1)S(1)} %collective-permute-done), channel_id=1, source_target_pairs={{0,1},{1,2},{2,3},{3,4},{4,5},{5,6},{6,7},{7,0},{8,9},{9,10},{10,1... | collective-permute-start | bytes 6291464 | tf_op jit(solution)/shard_map/ppermute | solution.py:156
  39.5 50.3 %collective-permute-start.4 = (bf16[16,512,128]{2,1,0:T(8,128)(2,1)S(1)}, bf16[16,512,128]{2,1,0:T(8,128)(2,1)}, u32[]{:S(2)}, u32[]{:S(2)}) collective-permute-start(bf16[16,512,128]{2,1,0:T(8,128)(2,1)S(1)} %convert_element_type.116), channel_id=1, source_target_pairs={{0,7},{1,0},{2,1},{3,2},{4,3},{5,4},{6,5},{7,6},{8,15},{9,8},{10,9... | collective-permute-start | bytes 6291464 | tf_op jit(solution)/shard_map/ppermute | solution.py:158
  89.8 49.9 %collective-permute-start.2 = (bf16[16,512,128]{2,1,0:T(8,128)(2,1)S(1)}, bf16[16,512,128]{2,1,0:T(8,128)(2,1)}, u32[]{:S(2)}, u32[]{:S(2)}) collective-permute-start(bf16[16,512,128]{2,1,0:T(8,128)(2,1)S(1)} %collective-permute-done.1), channel_id=1, source_target_pairs={{0,1},{1,2},{2,3},{3,4},{4,5},{5,6},{6,7},{7,0},{8,9},{9,10},{10,1... | collective-permute-start | bytes 6291464 | tf_op jit(solution)/shard_map/ppermute | solution.py:156
  89.8 51.9 %collective-permute-start.5 = (bf16[16,512,128]{2,1,0:T(8,128)(2,1)}, bf16[16,512,128]{2,1,0:T(8,128)(2,1)}, u32[]{:S(2)}, u32[]{:S(2)}) collective-permute-start(bf16[16,512,128]{2,1,0:T(8,128)(2,1)} %collective-permute-done.4), channel_id=1, source_target_pairs={{0,7},{1,0},{2,1},{3,2},{4,3},{5,4},{6,5},{7,6},{8,15},{9,8},{10,9... | collective-permute-start | bytes 6291464 | tf_op jit(solution)/shard_map/ppermute | solution.py:158
  139.7 48.4 %collective-permute-start.3 = (bf16[16,512,128]{2,1,0:T(8,128)(2,1)}, bf16[16,512,128]{2,1,0:T(8,128)(2,1)}, u32[]{:S(2)}, u32[]{:S(2)}) collective-permute-start(bf16[16,512,128]{2,1,0:T(8,128)(2,1)} %collective-permute-done.2), channel_id=1, source_target_pairs={{0,1},{1,2},{2,3},{3,4},{4,5},{5,6},{6,7},{7,0},{8,9},{9,10},{10,1... | collective-permute-start | bytes 6291464 | tf_op jit(solution)/shard_map/ppermute | solution.py:156
  139.7 5.6 copy-start.70
  140.1 7.1 copy-start.121
  141.7 58.6 %collective-permute-start.6 = (bf16[16,512,128]{2,1,0:T(8,128)(2,1)}, bf16[16,512,128]{2,1,0:T(8,128)(2,1)}, u32[]{:S(2)}, u32[]{:S(2)}) collective-permute-start(bf16[16,512,128]{2,1,0:T(8,128)(2,1)} %collective-permute-done.5), channel_id=1, source_target_pairs={{0,7},{1,0},{2,1},{3,2},{4,3},{5,4},{6,5},{7,6},{8,15},{9,8},{10,9... | collective-permute-start | bytes 6291464 | tf_op jit(solution)/shard_map/ppermute | solution.py:158
  145.9 350.1 %copy-start.99 = (f32[1,512]{1,0:T(1,128)}, f32[1,512]{1,0:T(1,128)S(1)}, u32[]{:S(2)}) copy-start(f32[1,512]{1,0:T(1,128)S(1)} %get-tuple-element.748) | copy-start | bytes 6148
  145.9 350.1 %copy-start.112 = (f32[1,512]{1,0:T(1,128)}, f32[1,512]{1,0:T(1,128)S(1)}, u32[]{:S(2)}) copy-start(f32[1,512]{1,0:T(1,128)S(1)} %get-tuple-element.747) | copy-start | bytes 6148
  277.9 75.4 %all-to-all-start = ((bf16[8,8,24576]{2,1,0:T(8,128)(2,1)}), bf16[8,8,24576]{2,1,0:T(8,128)(2,1)S(1)}, u32[]{:S(2)}, u32[]{:S(2)}) async-start(bf16[8,8,24576]{2,1,0:T(8,128)(2,1)} %reshape.599), calls=%async_computation | async-start | bytes 6291456 | tf_op jit(solution)/shard_map/all_to_all | solution.py:176
  457.9 30.1 %all-to-all-start.1 = ((bf16[1,8,8,8192]{3,1,0,2:T(8,128)(2,1)}), bf16[1,8,8,8192]{3,1,0,2:T(8,128)(2,1)S(1)}, u32[]{:S(2)}, u32[]{:S(2)}) async-start(bf16[1,8,8,8192]{3,1,0,2:T(8,128)(2,1)} %copy.213), calls=%async_computation.1 | async-start | bytes 2097152 | tf_op jit(solution)/shard_map/all_to_all | solution.py:187
  463.4 30.0 %copy-start.1 = (f32[1024,512]{0,1:T(8,128)}, f32[1024,512]{0,1:T(8,128)S(1)}, u32[]{:S(2)}) copy-start(f32[1024,512]{0,1:T(8,128)S(1)} %copy.262) | copy-start | bytes 6291460
  495.6 5.1 copy-start.8
  504.3 251.9 %copy-start.3 = (f32[1024,512]{0,1:T(8,128)}, f32[1024,512]{0,1:T(8,128)S(1)}, u32[]{:S(2)}) copy-start(f32[1024,512]{0,1:T(8,128)S(1)} %get-tuple-element.760) | copy-start | bytes 6291460
  539.6 76.2 %all-to-all-start.2 = ((bf16[8,8,24576]{2,1,0:T(8,128)(2,1)}), bf16[8,8,24576]{2,1,0:T(8,128)(2,1)}, u32[]{:S(2)}, u32[]{:S(2)}) async-start(bf16[8,8,24576]{2,1,0:T(8,128)(2,1)} %reshape.610), calls=%async_computation.2 | async-start | bytes 6291456 | tf_op jit(solution)/shard_map/all_to_all | solution.py:176
  720.4 30.5 %all-to-all-start.3 = ((bf16[1,8,8,8192]{3,1,0,2:T(8,128)(2,1)}), bf16[1,8,8,8192]{3,1,0,2:T(8,128)(2,1)S(1)}, u32[]{:S(2)}, u32[]{:S(2)}) async-start(bf16[1,8,8,8192]{3,1,0,2:T(8,128)(2,1)} %copy.223), calls=%async_computation.3 | async-start | bytes 2097152 | tf_op jit(solution)/shard_map/all_to_all | solution.py:187
  758.3 20.3 %copy-start.13 = (f32[1024,512]{0,1:T(8,128)}, f32[1024,512]{0,1:T(8,128)S(1)}, u32[]{:S(2)}) copy-start(f32[1024,512]{0,1:T(8,128)S(1)} %get-tuple-element.762) | copy-start | bytes 6291460
  758.4 20.2 %copy-start.87 = (f32[1024]{0:T(1024)}, f32[1024]{0:T(1024)S(1)}, u32[]{:S(2)}) copy-start(f32[1024]{0:T(1024)S(1)} %broadcast_multiply_fusion.1) | copy-start | bytes 12292
  758.7 19.9 %copy-start.104 = (f32[1024]{0:T(1024)}, f32[1024]{0:T(1024)S(1)}, u32[]{:S(2)}) copy-start(f32[1024]{0:T(1024)S(1)} %fusion.118) | copy-start | bytes 12292
  760.7 6.5 copy-start.49
  760.7 6.5 copy-start.58
  767.2 7.9 copy-start.128
  787.0 30.3 %all-to-all-start.4 = ((bf16[8,8,8192]{2,1,0:T(8,128)(2,1)}), bf16[8,8,8192]{2,1,0:T(8,128)(2,1)S(1)}, u32[]{:S(2)}, u32[]{:S(2)}) async-start(bf16[8,8,8192]{2,1,0:T(8,128)(2,1)} %reshape.622), calls=%async_computation.4 | async-start | bytes 2097152 | tf_op jit(solution)/shard_map/all_to_all | solution.py:242
  1148.3 6.3 copy-start.30
  1164.3 10.4 copy-start.22
  1164.3 10.4 copy-start.51
  1193.8 30.1 %all-to-all-start.6 = ((bf16[8,8,8192]{2,1,0:T(8,128)(2,1)}), bf16[8,8,8192]{2,1,0:T(8,128)(2,1)S(1)}, u32[]{:S(2)}, u32[]{:S(2)}) async-start(bf16[8,8,8192]{2,1,0:T(8,128)(2,1)} %reshape.628), calls=%async_computation.6 | async-start | bytes 2097152 | tf_op jit(solution)/shard_map/all_to_all | solution.py:242
  1470.8 76.1 %all-to-all-start.7 = ((bf16[1,8,8,24576]{3,1,0,2:T(8,128)(2,1)}), bf16[1,8,8,24576]{3,1,0,2:T(8,128)(2,1)}, u32[]{:S(2)}, u32[]{:S(2)}) async-start(bf16[1,8,8,24576]{3,1,0,2:T(8,128)(2,1)} %copy.245), calls=%async_computation.7 | async-start | bytes 6291456 | tf_op jit(solution)/shard_map/all_to_all | solution.py:260
  1475.4 364.6 %reduce-scatter.2.cloned.1.call-start = ((), (), s32[]{:S(2)}) async-start(), calls=%async_computation.9 | async-start | bytes 25952256 | tf_op jit(solution)/shard_map/reduce_scatter | solution.py:278
  1477.4 6.6 copy-start.14
  1477.4 6.6 copy-start.88
  1477.4 6.6 copy-start.105
  1477.4 6.6 copy-start.108
  1477.4 6.6 copy-start.115
  1484.0 6.9 copy-start.31
  1595.6 247.3 %copy-start.122 = (s32[96]{0:T(128)S(1)}, s32[96]{0:T(128)}, u32[]{:S(2)}) copy-start(s32[96]{0:T(128)} %copy-done.121) | copy-start | bytes 1156
  1595.6 247.3 %copy-start.123 = (pred[96]{0:T(512)(128)(4,1)S(1)}, pred[96]{0:T(512)(128)(4,1)}, u32[]{:S(2)}) copy-start(pred[96]{0:T(512)(128)(4,1)} %get-tuple-element.756) | copy-start | bytes 292
  1595.6 345.7 %all-gather.2.cloned.1.call-start = ((), (), s32[]{:S(2)}) async-start(), calls=%async_computation.10 | async-start | bytes 12976128 | tf_op jit(solution)/shard_map/all_gather | solution.py:283
  1869.6 47.6 %copy-start.71 = (f32[8,512]{1,0:T(8,128)S(1)}, f32[8,512]{1,0:T(8,128)}, u32[]{:S(2)}) copy-start(f32[8,512]{1,0:T(8,128)} %param.33) | copy-start | bytes 49156
  1869.6 47.6 %copy-start.102 = (f32[8,512]{1,0:T(8,128)S(1)}, f32[8,512]{1,0:T(8,128)}, u32[]{:S(2)}) copy-start(f32[8,512]{1,0:T(8,128)} %param.35) | copy-start | bytes 49156
  1869.6 47.6 %copy-start.103 = (f32[8,512]{1,0:T(8,128)S(1)}, f32[8,512]{1,0:T(8,128)}, u32[]{:S(2)}) copy-start(f32[8,512]{1,0:T(8,128)} %param.34) | copy-start | bytes 49156
  1966.6 9.6 copy-start.27
  1966.6 10.5 copy-start.28
  1976.2 5.6 copy-start.29
  (111 other events, 316.4 us)
Sparse Core Ops, SparseCore 0:
  1595.8 244.1 reduce-scatter.1
  1843.9 97.3 all-gather.1
